TPU v7x, 32 devices: a whole 2x2x4 slice. The times are simulated.
32 devices in a mesh: dp: 2 (over y), row: 4 (over z), col: 4 (over x, core).
Axes of the slice: x: 2, y: 2, z: 4, core: 2. Of those that a mesh axis runs over, the one named last changes fastest.
Arguments:
- inputs: bfloat16 [2, 256, 128, 512], P('dp', None, 'row', 'col'), may hold values from -6 to 6
- reduce_weight: bfloat16 [64, 256], replicated, may hold values from -0.375 to 0.375
- spatial_weight: bfloat16 [3, 3, 64, 64], replicated, may hold values from -0.25 to 0.25
- expand_weight: bfloat16 [256, 64], replicated, may hold values from -0.75 to 0.75
- class_weight: bfloat16 [3, 3, 135, 256], replicated, may hold values from -0.125 to 0.125
- anchor_labels: int32 [2, 9, 128, 512], P('dp', None, 'row', 'col'), may hold values from 0 to 15, as said below
- anchor_mask: int32 [2, 9, 128, 512], P('dp', None, 'row', 'col'), may hold values from 0 to 1, as said below
Outputs:
- loss: float32 [], replicated
- grad_reduce: float32 [64, 256], replicated
- grad_spatial: float32 [3, 3, 64, 64], replicated
- grad_expand: float32 [256, 64], replicated
- grad_class: float32 [3, 3, 135, 256], replicated
Inputs may be any that keep to these rules, and one draw needn't show every extreme that they name: `anchor_labels`: labels are 0 to 15; anchor 0 at the first row and column of every tile is positive. `anchor_mask`: every anchor with a label above 0 has mask 1.
All inputs are finite; a program needn't handle non-finite values.
Results may differ from a plain program's by a relative error of at most 0.0034.
Values may be sent and summed in bfloat16 or wider, within the bound.
A program may use at most 128 MiB of HBM per device.

v0:
```python
import functools

import jax
import jax.numpy as jnp
import numpy as np
from jax import lax
from jax.experimental import pallas as pl
from jax.experimental.pallas import tpu as pltpu
from jax.sharding import PartitionSpec as P

A = 9
K = 15
HALO = 4
STEP = 512
EDGE = 256
F32 = jnp.float32
BF16 = jnp.bfloat16
AXES = ("dp", "row", "col")


def extended(cells, sides, width):
    for axis, dim in sides:
        count = lax.axis_size(axis)
        ends = count - 1
        head = lax.slice_in_dim(cells, 0, width, axis=dim)
        tail = lax.slice_in_dim(cells, cells.shape[dim] - width, cells.shape[dim], axis=dim)
        cells = jnp.concatenate(
            [
                lax.ppermute(tail, axis, [(i, (i + 1) % count) for i in range(ends)]),
                cells,
                lax.ppermute(head, axis, [((i + 1) % count, i) for i in range(ends)]),
            ],
            axis=dim,
        )
    return cells


def dot(a, b):
    return jnp.dot(a, b, preferred_element_type=F32)


def dot_t(a, b):
    return lax.dot_general(a, b, (((1,), (1,)), ((), ())), preferred_element_type=F32)


def tile_kernel(
    pitch, geo,
    x_ref, own_ref, spread_ref, wr_ref, ws_ref, wsb_ref, we_ref, wet_ref, wc_ref, wcb_ref,
    reduce_ref, spatial_ref, expand_ref, class_ref, focal_ref, count_ref,
    first, second, block, dlog, dsec, big, small, acc_c,
):
    chans = we_ref.shape[0]
    mid = we_ref.shape[1]
    outs = wc_ref.shape[0]
    length = x_ref.shape[1]
    shifts = [(dy - 1) * pitch + (dx - 1) for dy in range(3) for dx in range(3)]

    def columns(ref, base, sign, dest):
        rows = ref.shape[0]
        window = ref[:, pl.ds(base, STEP + 2 * EDGE)]
        for tap, shift in enumerate(shifts):
            at = EDGE + sign * shift
            dest[tap * rows:(tap + 1) * rows, :] = window[:, at:at + STEP]

    def at(i, start):
        return pl.multiple_of(start + i * STEP, 128)

    def loop(start, steps, body, init=0):
        return lax.fori_loop(0, steps, lambda i, c: body(at(i, start), c), init)

    first[:, :EDGE] = jnp.zeros((mid, EDGE), BF16)
    first[:, EDGE + length:] = jnp.zeros((mid, EDGE), BF16)
    dlog[...] = jnp.zeros_like(dlog)
    acc_c[...] = jnp.zeros_like(acc_c)
    reduce_ref[...] = jnp.zeros_like(reduce_ref)
    spatial_ref[...] = jnp.zeros_like(spatial_ref)
    expand_ref[...] = jnp.zeros_like(expand_ref)

    def make_first(p, c):
        z = dot(wr_ref[...], x_ref[:chans, pl.ds(p, STEP)])
        first[:, pl.ds(pl.multiple_of(p + EDGE, 128), STEP)] = jnp.maximum(z, 0.0).astype(BF16)
        return c

    loop(0, length // STEP, make_first)

    def make_block(p, c):
        columns(first, p, 1, small)
        s = jnp.maximum(dot(ws_ref[...], small[...]), 0.0).astype(BF16)
        second[:, pl.ds(p, STEP)] = s
        xs = x_ref[:, pl.ds(p, STEP)]
        valid = xs[chans + A:chans + A + 1].astype(F32)
        b = jnp.maximum(xs[:chans].astype(F32) + dot(we_ref[...], s), 0.0) * valid
        block[:, pl.ds(p, STEP)] = b.astype(BF16)
        return c

    loop(0, length // STEP, make_block)

    ident = lax.rem(lax.broadcasted_iota(jnp.int32, (outs, 1), 0), K) + 1

    def make_dlog(p, carry):
        total, count = carry
        columns(block, pl.multiple_of(p - EDGE, 128), 1, big)
        z = dot(wc_ref[...], big[...])
        code = x_ref[chans:, pl.ds(p, STEP)]
        own = own_ref[:, pl.ds(p, STEP)]
        wide = dot(spread_ref[...], code)
        live = wide >= 15.5
        label = jnp.where(live, wide - 16.0, wide)
        target = label == ident.astype(F32)
        alpha = jnp.where(target, 0.25, 0.75)
        alpha = jnp.where(live, alpha, 0.0)
        u = jnp.where(target, -z, z)
        e = jnp.exp(-jnp.abs(u))
        inv = 1.0 / (1.0 + e)
        low = e * inv
        pos = u >= 0.0
        prob = jnp.where(pos, inv, low)
        rest = jnp.where(pos, low, inv)
        soft = jnp.maximum(u, 0.0) + jnp.log1p(e)
        scaled = alpha * prob * prob
        total = total + jnp.sum(scaled * soft, axis=0, keepdims=True) * own
        slope = scaled * (2.0 * rest * soft + prob)
        d = jnp.where(target, -slope, slope).astype(BF16)
        dlog[:, pl.ds(p, STEP)] = d
        mine = (d.astype(F32) * own).astype(BF16)
        acc_c[...] += dot_t(mine, big[...])
        codes = code.astype(F32)
        labels = jnp.where(codes >= 15.5, codes - 16.0, codes)
        row = lax.broadcasted_iota(jnp.int32, codes.shape, 0)
        hit = jnp.where((labels > 0.5) & (row < A), 1.0, 0.0)
        count = count + jnp.sum(hit, axis=0, keepdims=True) * own
        return total, count

    zero = jnp.zeros((1, STEP), F32)
    total, count = loop(geo[0][0], geo[0][1], make_dlog, (zero, zero))
    focal_ref[...] = jnp.sum(total, keepdims=True).reshape(1, 1)
    count_ref[...] = jnp.sum(count, keepdims=True).reshape(1, 1)

    def make_dsec(p, c):
        columns(dlog, pl.multiple_of(p - EDGE, 128), -1, big.at[:9 * outs])
        g = dot(wcb_ref[...], big[:9 * outs, :])
        b = block[:, pl.ds(p, STEP)].astype(F32)
        ds = jnp.where(b > 0.0, g, 0.0).astype(BF16)
        s = second[:, pl.ds(p, STEP)]
        own = own_ref[:, pl.ds(p, STEP)]
        sf = s.astype(F32)
        expand_ref[...] += dot_t(ds, (sf * own).astype(BF16))
        h = dot(wet_ref[...], ds)
        dsec[:, pl.ds(p, STEP)] = jnp.where(sf > 0.0, h, 0.0).astype(BF16)
        return c

    loop(geo[0][0], geo[0][1], make_dsec)

    def make_dfirst(p, c):
        own = own_ref[:, pl.ds(p, STEP)]
        columns(first, p, 1, small)
        mine = (dsec[:, pl.ds(p, STEP)].astype(F32) * own).astype(BF16)
        spatial_ref[...] += dot_t(mine, small[...])
        columns(dsec, pl.multiple_of(p - EDGE, 128), -1, small)
        g = dot(wsb_ref[...], small[...]) * own
        f = first[:, pl.ds(pl.multiple_of(p + EDGE, 128), STEP)].astype(F32)
        df = jnp.where(f > 0.0, g, 0.0).astype(BF16)
        reduce_ref[...] += dot_t(df, x_ref[:chans, pl.ds(p, STEP)])
        return c

    loop(geo[1][0], geo[1][1], make_dfirst)
    for tap in range(9):
        class_ref[tap] = acc_c[:, tap * chans:(tap + 1) * chans]


def per_device(
    inputs, reduce_weight, spatial_weight, expand_weight, class_weight, anchor_labels, anchor_mask
):
    tiles, chans, rows, cols = inputs.shape
    mid = reduce_weight.shape[0]
    heads = class_weight.shape[2]
    outs = -(-heads // 16) * 16
    tall, pitch = rows + 2 * HALO, cols + 2 * HALO
    pixels = tall * pitch
    length = -(-pixels // STEP) * STEP

    def span(margin):
        low = margin * pitch + margin
        high = (tall - margin) * pitch
        start = max(EDGE, low // 128 * 128 // EDGE * EDGE)
        return start, -(-(high - start) // STEP)

    geo = (span(2), span(4))
    need = geo[0][0] + geo[0][1] * STEP + EDGE
    length = max(length, -(-need // STEP) * STEP)

    code = (anchor_labels + 16 * anchor_mask).astype(BF16)
    ones = jnp.ones((tiles, 1, rows, cols), BF16)
    none = jnp.zeros((tiles, 16 - A - 1, rows, cols), BF16)
    field = jnp.concatenate([inputs, code, ones, none], axis=1)
    field = extended(field, (("row", 2), ("col", 3)), HALO)
    field = field.reshape(tiles, chans + 16, pixels)
    field = jnp.pad(field, ((0, 0), (0, 0), (0, length - pixels)))

    own = np.zeros((tall, pitch), np.float32)
    own[HALO:HALO + rows, HALO:HALO + cols] = 1.0
    own = jnp.asarray(np.pad(own.reshape(1, pixels), ((0, 0), (0, length - pixels))))
    spread = np.zeros((outs, 16), np.float32)
    spread[np.arange(heads), np.arange(heads) // K] = 1.0
    spread = jnp.asarray(spread, BF16)

    ws = spatial_weight.transpose(2, 0, 1, 3).reshape(mid, 9 * mid)
    wsb = spatial_weight.transpose(3, 0, 1, 2).reshape(mid, 9 * mid)
    wide = jnp.pad(class_weight, ((0, 0), (0, 0), (0, outs - heads), (0, 0)))
    wc = wide.transpose(2, 0, 1, 3).reshape(outs, 9 * chans)
    wcb = wide.transpose(3, 0, 1, 2).reshape(chans, 9 * outs)

    call = pl.pallas_call(
        functools.partial(tile_kernel, pitch, geo),
        out_shape=(
            jax.ShapeDtypeStruct((mid, chans), F32),
            jax.ShapeDtypeStruct((mid, 9 * mid), F32),
            jax.ShapeDtypeStruct((chans, mid), F32),
            jax.ShapeDtypeStruct((9, outs, chans), F32),
            jax.ShapeDtypeStruct((1, 1), F32),
            jax.ShapeDtypeStruct((1, 1), F32),
        ),
        in_specs=[pl.BlockSpec(memory_space=pltpu.VMEM)] * 10,
        out_specs=[pl.BlockSpec(memory_space=pltpu.VMEM)] * 6,
        scratch_shapes=[
            pltpu.VMEM((mid, length + 2 * EDGE), BF16),
            pltpu.VMEM((mid, length), BF16),
            pltpu.VMEM((chans, length), BF16),
            pltpu.VMEM((outs, length), BF16),
            pltpu.VMEM((mid, length), BF16),
            pltpu.VMEM((9 * chans, STEP), BF16),
            pltpu.VMEM((9 * mid, STEP), BF16),
            pltpu.VMEM((outs, 9 * chans), F32),
        ],
        compiler_params=pltpu.CompilerParams(vmem_limit_bytes=50 * 1024 * 1024),
        name="tile_step",
    )
    sums = None
    for t in range(tiles):
        part = call(
            field[t], own, spread, reduce_weight, ws, wsb, expand_weight, expand_weight.T, wc, wcb
        )
        sums = part if sums is None else tuple(a + b for a, b in zip(sums, part))
    return finish(sums, mid, heads)


def finish(sums, mid, heads):
    reduce_sum, spatial_sum, expand_sum, class_sum, focal, count = lax.psum(sums, AXES)
    chans = reduce_sum.shape[1]
    count = count[0, 0]
    scale = 1.0 / count
    spatial = spatial_sum.reshape(mid, 3, 3, mid).transpose(1, 2, 0, 3)
    return (
        focal[0, 0] / count,
        reduce_sum * scale,
        spatial * scale,
        expand_sum * scale,
        class_sum[:, :heads].reshape(3, 3, heads, chans) * scale,
    )


def solution(mesh):
    tiled = P("dp", None, "row", "col")
    return jax.shard_map(
        per_device,
        mesh=mesh,
        in_specs=(tiled, P(), P(), P(), P(), tiled, tiled),
        out_specs=(P(), P(), P(), P(), P()),
        check_vma=False,
    )
```

profile of v0, /device:TPU:0, one launch (start us, length us, event | category | flops | bytes accessed | tf_op | source)
XLA Modules:
  0.0 289.9 jit_solution(14990084708624896661)
XLA Ops:
  7.2 2.4 copy.50
  9.6 1.3 add_convert_fusion
  11.1 5.0 %collective-permute-start = (bf16[1,272,4,128]{3,1,2,0:T(8,128)(2,1)S(1)}, bf16[1,272,4,128]{3,1,2,0:T(8,128)(2,1)S(1)}, u32[]{:S(2)}, u32[]{:S(2)}) collective-permute-start(bf16[1,272,4,128]{3,1,2,0:T(8,128)(2,1)S(1)} %get-tuple-element.45), channel_id=1, source_target_pairs={{0,4},{4,8},{8,12},{1,5},{5,9},{9,13},{2,6},{6,10},{10,14},{3,7},{... | collective-permute-start | bytes 835592 | tf_op jit(solution)/shard_map/ppermute | solution.py:29
  16.1 1.3 collective-permute-start.1
  17.4 4.6 %collective-permute-done = bf16[1,272,4,128]{3,1,2,0:T(8,128)(2,1)S(1)} collective-permute-done((bf16[1,272,4,128]{3,1,2,0:T(8,128)(2,1)S(1)}, bf16[1,272,4,128]{3,1,2,0:T(8,128)(2,1)S(1)}, u32[]{:S(2)}, u32[]{:S(2)}) %collective-permute-start) | collective-permute-done | bytes 278560 | tf_op jit(solution)/shard_map/ppermute | solution.py:29
  22.0 4.1 %collective-permute-done.1 = bf16[1,272,4,128]{3,1,2,0:T(8,128)(2,1)S(1)} collective-permute-done((bf16[1,272,4,128]{3,1,2,0:T(8,128)(2,1)S(1)}, bf16[1,272,4,128]{3,1,2,0:T(8,128)(2,1)S(1)}, u32[]{:S(2)}, u32[]{:S(2)}) %collective-permute-start.1) | collective-permute-done | bytes 278560 | tf_op jit(solution)/shard_map/ppermute | solution.py:31
  26.1 2.8 pad_maximum_fusion.1
  29.0 2.5 fusion
  31.5 4.0 %copy.52 = bf16[1,272,40,4]{1,2,3,0:T(8,128)(2,1)} copy(bf16[1,272,40,4]{3,1,2,0:T(8,128)(2,1)} %get-tuple-element.43) | data formatting | bytes 174080 | tf_op jit(solution)/shard_map/slice | solution.py:26
  35.5 2.1 collective-permute-start.2
  37.6 2.7 copy.53
  40.3 1.6 collective-permute-start.3
  41.9 1.2 fusion.1
  43.1 0.5 copy.59
  43.5 0.8 reshape.37.wc_ref
  44.3 0.3 copy.63.wcb_ref
  45.3 3.6 %copy.54 = bf16[1,272,40,4]{3,1,2,0:T(8,128)(2,1)} copy(bf16[1,272,40,4]{1,2,3,0:T(8,128)(2,1)} %collective-permute-done.2) | data formatting | bytes 174080 | tf_op jit(solution)/shard_map/ppermute | solution.py:29
  48.9 2.9 copy.55
  51.8 15.3 %pad_maximum_fusion = bf16[1,272,40,136]{3,1,2,0:T(8,128)(2,1)} fusion(bf16[1,272,40,4]{3,1,2,0:T(8,128)(2,1)} %copy.55, bf16[1,272,4,128]{3,1,2,0:T(8,128)(2,1)S(1)} %collective-permute-done.1, bf16[1,6,32,128]{3,1,2,0:T(8,128)(2,1)S(1)} %copy-done.6, bf16[1,1,32,128]{3,1,2,0:T(2,128)(2,1)S(1)} %broadcast_in_dim.6, bf16[1,9,32,128]{3,1,2,0:T(8,128)(2,1)S(1)} %copy.51, ...), kind=kLoop, calls=%fused_computation | loop fusion | flops 23674880 | bytes 5918720 | tf_op jit(solution)/shard_map/concatenate | solution.py:27
  67.1 7.7 %copy.56 = bf16[1,272,40,136]{1,3,2,0:T(8,128)(2,1)} copy(bf16[1,272,40,136]{3,1,2,0:T(8,128)(2,1)} %pad_maximum_fusion) | data formatting | bytes 5918720 | tf_op jit(solution)/shard_map/concatenate | solution.py:27
  74.9 5.9 %copy.57 = bf16[1,272,5440]{2,1,0:T(8,128)(2,1)} copy(bf16[1,272,5440]{1,2,0:T(8,128)(2,1)} %bitcast.21) | data formatting | bytes 5918720 | tf_op jit(solution)/shard_map/reshape | solution.py:197
  80.7 3.7 %pad_bitcast_fusion.x_ref = bf16[272,5632]{1,0:T(8,128)(2,1)} fusion(bf16[1,272,5440]{2,1,0:T(8,128)(2,1)} %copy.57), kind=kLoop, calls=%fused_computation.1 | loop fusion | bytes 6023168 | tf_op jit(solution)/shard_map/squeeze | solution.py:241
  84.4 52.9 %tile_step.1 = (f32[64,256]{1,0:T(8,128)}, f32[64,576]{1,0:T(8,128)}, f32[256,64]{1,0:T(8,128)}, f32[9,144,256]{2,1,0:T(8,128)}, f32[1,1]{1,0:T(1,128)}, /*index=5*/f32[1,1]{1,0:T(1,128)}) custom-call(bf16[272,5632]{1,0:T(8,128)(2,1)} %pad_bitcast_fusion.x_ref, f32[1,5632]{1,0:T(1,128)S(1)} %copy-done.3, bf16[144,16]{1,0:T(8,128)(2,1)S(1)} %copy-done.1, ...), custom_call_target="tpu_custom_call" | custom-call | tf_op jit(solution)/shard_map/tile_step/pallas_call | solution.py:240
  137.3 43.4 %all-reduce.2 = (f32[1,1]{1,0:T(1,128)}, f32[1,1]{1,0:T(1,128)}) all-reduce(f32[1,1]{1,0:T(1,128)} %get-tuple-element.11, f32[1,1]{1,0:T(1,128)} %get-tuple-element.12), channel_id=1, replica_groups=mesh['dp'=2,'row'=4,'col'=4] {'dp','row','col'}, use_global_device_ids=true, to_apply=%region_0.1 | all-reduce | flops 2 | bytes 16 | tf_op jit(solution)/shard_map/psum | solution.py:248
  182.7 91.8 %all-reduce.6.cloned.1.call-done = (f32[64,256]{1,0:T(8,128)}, f32[64,576]{1,0:T(8,128)}, f32[256,64]{1,0:T(8,128)}, f32[9,144,256]{2,1,0:T(8,128)}) async-done(((f32[64,256]{1,0:T(8,128)}, f32[64,576]{1,0:T(8,128)}, f32[256,64]{1,0:T(8,128)}, f32[9,144,256]{2,1,0:T(8,128)}), (f32[64,256]{1,0:T(8,128)}, f32[64,576]{1,0:T(8,128)}, f32[256,64]{1,0:T(8,128)}, ...) | async-done | bytes 1605648 | tf_op jit(solution)/shard_map/psum | solution.py:248
  274.5 2.4 slice_multiply_fusion
  276.9 0.9 broadcast_multiply_fusion.1
  277.8 0.7 copy.66
  278.5 0.9 broadcast_multiply_fusion
  279.5 0.1 copy.64
  279.6 0.9 copy.65
  280.5 1.5 broadcast_multiply_fusion.2
  (28 shorter events, 0.8 us)
Async XLA Ops:
  7.2 267.3 %all-reduce.6.cloned.1.call-start = ((), (), s32[]{:S(2)}) async-start(), calls=%async_computation | async-start | bytes 3375104 | tf_op jit(solution)/shard_map/psum | solution.py:248
  9.6 16.5 %copy-start.4 = (bf16[1,256,32,128]{3,1,2,0:T(8,128)(2,1)}, bf16[1,256,32,128]{3,1,2,0:T(8,128)(2,1)S(1)}, u32[]{:S(2)}) copy-start(bf16[1,256,32,128]{3,1,2,0:T(8,128)(2,1)S(1)} %copy.50) | copy-start | bytes 6291460
  11.0 15.1 %copy-start.5 = (bf16[1,6,32,128]{3,1,2,0:T(8,128)(2,1)}, bf16[1,6,32,128]{3,1,2,0:T(8,128)(2,1)S(1)}, u32[]{:S(2)}) copy-start(bf16[1,6,32,128]{3,1,2,0:T(8,128)(2,1)S(1)} %broadcast_in_dim.7) | copy-start | bytes 147460
  11.1 10.9 %collective-permute-start = (bf16[1,272,4,128]{3,1,2,0:T(8,128)(2,1)S(1)}, bf16[1,272,4,128]{3,1,2,0:T(8,128)(2,1)S(1)}, u32[]{:S(2)}, u32[]{:S(2)}) collective-permute-start(bf16[1,272,4,128]{3,1,2,0:T(8,128)(2,1)S(1)} %get-tuple-element.45), channel_id=1, source_target_pairs={{0,4},{4,8},{8,12},{1,5},{5,9},{9,13},{2,6},{6,10},{10,14},{3,7},{... | collective-permute-start | bytes 835592 | tf_op jit(solution)/shard_map/ppermute | solution.py:29
  16.1 10.0 %collective-permute-start.1 = (bf16[1,272,4,128]{3,1,2,0:T(8,128)(2,1)S(1)}, bf16[1,272,4,128]{3,1,2,0:T(8,128)(2,1)S(1)}, u32[]{:S(2)}, u32[]{:S(2)}) collective-permute-start(bf16[1,272,4,128]{3,1,2,0:T(8,128)(2,1)S(1)} %get-tuple-element.46), channel_id=1, source_target_pairs={{4,0},{8,4},{12,8},{5,1},{9,5},{13,9},{6,2},{10,6},{14,10},{7,3},{... | collective-permute-start | bytes 835592 | tf_op jit(solution)/shard_map/ppermute | solution.py:31
  35.5 9.6 %copy-start = (bf16[256,64]{0,1:T(8,128)(2,1)S(1)}, bf16[256,64]{0,1:T(8,128)(2,1)}, u32[]{:S(2)}) copy-start(bf16[256,64]{0,1:T(8,128)(2,1)} %param.12) | copy-start | bytes 98308
  35.5 9.8 %collective-permute-start.2 = (bf16[1,272,40,4]{1,2,3,0:T(8,128)(2,1)}, bf16[1,272,40,4]{1,2,3,0:T(8,128)(2,1)}, u32[]{:S(2)}, u32[]{:S(2)}) collective-permute-start(bf16[1,272,40,4]{1,2,3,0:T(8,128)(2,1)} %copy.52), channel_id=1, source_target_pairs={{0,1},{1,2},{2,3},{4,5},{5,6},{6,7},{8,9},{9,10},{10,11},{12,13},{... | collective-permute-start | bytes 261128 | tf_op jit(solution)/shard_map/ppermute | solution.py:29
  40.3 4.4 %copy-start.7 = (bf16[3,3,64,64]{3,2,1,0:T(8,128)(2,1)S(1)}, bf16[3,3,64,64]{3,2,1,0:T(8,128)(2,1)}, u32[]{:S(2)}) copy-start(bf16[3,3,64,64]{3,2,1,0:T(8,128)(2,1)} %param.11) | copy-start | bytes 221188
  40.3 8.6 %collective-permute-start.3 = (bf16[1,272,40,4]{1,2,3,0:T(8,128)(2,1)}, bf16[1,272,40,4]{1,2,3,0:T(8,128)(2,1)S(1)}, u32[]{:S(2)}, u32[]{:S(2)}) collective-permute-start(bf16[1,272,40,4]{1,2,3,0:T(8,128)(2,1)} %copy.53), channel_id=1, source_target_pairs={{1,0},{2,1},{3,2},{5,4},{6,5},{7,6},{9,8},{10,9},{11,10},{13,12},{... | collective-permute-start | bytes 261128 | tf_op jit(solution)/shard_map/ppermute | solution.py:31
  43.1 8.7 %copy-start.6 = (bf16[1,6,32,128]{3,1,2,0:T(8,128)(2,1)S(1)}, bf16[1,6,32,128]{3,1,2,0:T(8,128)(2,1)}, u32[]{:S(2)}) copy-start(bf16[1,6,32,128]{3,1,2,0:T(8,128)(2,1)} %copy-done.5) | copy-start | bytes 147460
  74.9 9.5 %copy-start.1 = (bf16[144,16]{1,0:T(8,128)(2,1)S(1)}, bf16[144,16]{1,0:T(8,128)(2,1)}, u32[]{:S(2)}) copy-start(bf16[144,16]{1,0:T(8,128)(2,1)} %constant.16.clone.spread_ref) | copy-start | bytes 13828
  74.9 9.5 %copy-start.2 = (bf16[64,256]{1,0:T(8,128)(2,1)S(1)}, bf16[64,256]{1,0:T(8,128)(2,1)}, u32[]{:S(2)}) copy-start(bf16[64,256]{1,0:T(8,128)(2,1)} %wr_ref.1) | copy-start | bytes 98308
  74.9 9.5 %copy-start.3 = (f32[1,5632]{1,0:T(1,128)S(1)}, f32[1,5632]{1,0:T(1,128)}, u32[]{:S(2)}) copy-start(f32[1,5632]{1,0:T(1,128)} %constant.15.clone.own_ref) | copy-start | bytes 67588
Sparse Core Ops, SparseCore 0:
  137.4 137.0 all-reduce.5
where the time goes:
time: 291 us; the launch traced here: 290 us
  waiting for transfers between devices  101 us (35%)
  Pallas kernels  52.9 us (18%)
  blocking collectives  43.4 us (15%)
  local copies, waits for them, and re-layouts  40.6 us (14%)
  other arithmetic  25.3 us (9%)
  between operations  17.3 us (6%)
  starting transfers between devices  9.96 us (3%)
    psum x1, waiting for transfers between devices, finish(): lax.psum(sums, AXES)  91.8 us
    pallas_call x1, Pallas kernels, per_device(): call(field[t], own, spread, reduce_weight, ws, wsb, expand_weight, expand...  52.9 us
    psum x1, blocking collectives, finish(): lax.psum(sums, AXES)  43.4 us
    concatenate x2, other arithmetic, extended(): jnp.concatenate([lax.ppermute(tail, axis, [(i, (i + 1) % count) for i in...  18.2 us
    concatenate x1, local copies, waits for them, and re-layouts, extended(): jnp.concatenate([lax.ppermute(tail, axis, [(i, (i + 1) % count) for i in...  7.74 us
    ppermute x2, starting transfers between devices, extended(): lax.ppermute(tail, axis, [(i, (i + 1) % count) for i in range(ends)])  7.04 us
    slice x2, local copies, waits for them, and re-layouts, extended(): lax.slice_in_dim(cells, cells.shape[dim] - width, cells.shape[dim], axis=...  6.52 us
    reshape x1, local copies, waits for them, and re-layouts, per_device(): field = field.reshape(tiles, chans + 16, pixels)  5.87 us
  transfers between devices with their start and end apart: 5, of which 3 were waited for; matrix products, arithmetic and copies ran while one was open for 3% of the time, Pallas kernels for 0%

commit v1 on v0

--- a/solution.py
+++ b/solution.py
@@ -44,10 +44,10 @@
 
 
 def tile_kernel(
-    pitch, geo,
-    x_ref, own_ref, spread_ref, wr_ref, ws_ref, wsb_ref, we_ref, wet_ref, wc_ref, wcb_ref,
-    reduce_ref, spatial_ref, expand_ref, class_ref, focal_ref, count_ref,
-    first, second, block, dlog, dsec, big, small, acc_c,
+    pitch, geo, heads_in,
+    mid_ref, left_ref, right_ref, own_ref, spread_ref, wr_ref, ws_ref, wsb_ref, we_ref, wet_ref, wc_ref, wcb_ref,
+    pack_ref, stat_ref,
+    x_ref, first, second, block, dlog, dsec, big, small, acc_c, reduce_ref, spatial_ref, expand_ref,
 ):
     chans = we_ref.shape[0]
     mid = we_ref.shape[1]
@@ -67,6 +67,15 @@
 
     def loop(start, steps, body, init=0):
         return lax.fori_loop(0, steps, lambda i, c: body(at(i, start), c), init)
+
+    tall, _, cols = mid_ref.shape
+    x_ref[:, tall * pitch // 128 * 128:] = jnp.zeros(
+        (x_ref.shape[0], length - tall * pitch // 128 * 128), BF16
+    )
+    for h in range(tall):
+        x_ref[:, h * pitch:h * pitch + HALO] = left_ref[h]
+        x_ref[:, h * pitch + HALO:h * pitch + HALO + cols] = mid_ref[h]
+        x_ref[:, h * pitch + HALO + cols:(h + 1) * pitch] = right_ref[h]
 
     first[:, :EDGE] = jnp.zeros((mid, EDGE), BF16)
     first[:, EDGE + length:] = jnp.zeros((mid, EDGE), BF16)
@@ -133,8 +142,9 @@
 
     zero = jnp.zeros((1, STEP), F32)
     total, count = loop(geo[0][0], geo[0][1], make_dlog, (zero, zero))
-    focal_ref[...] = jnp.sum(total, keepdims=True).reshape(1, 1)
-    count_ref[...] = jnp.sum(count, keepdims=True).reshape(1, 1)
+    stat_ref[0:1, :] = sum(total[:, k * 128:(k + 1) * 128] for k in range(STEP // 128))
+    stat_ref[1:2, :] = sum(count[:, k * 128:(k + 1) * 128] for k in range(STEP // 128))
+    stat_ref[2:, :] = jnp.zeros((6, 128), F32)
 
     def make_dsec(p, c):
         columns(dlog, pl.multiple_of(p - EDGE, 128), -1, big.at[:9 * outs])
@@ -144,7 +154,7 @@
         s = second[:, pl.ds(p, STEP)]
         own = own_ref[:, pl.ds(p, STEP)]
         sf = s.astype(F32)
-        expand_ref[...] += dot_t(ds, (sf * own).astype(BF16))
+        expand_ref[...] += dot_t((sf * own).astype(BF16), ds)
         h = dot(wet_ref[...], ds)
         dsec[:, pl.ds(p, STEP)] = jnp.where(sf > 0.0, h, 0.0).astype(BF16)
         return c
@@ -164,8 +174,146 @@
         return c
 
     loop(geo[1][0], geo[1][1], make_dfirst)
+    heads = heads_in
+    spots = layout(mid, heads)[:3]
+    pack_ref[...] = jnp.zeros_like(pack_ref)
     for tap in range(9):
-        class_ref[tap] = acc_c[:, tap * chans:(tap + 1) * chans]
+        pack_ref[tap * heads:(tap + 1) * heads, :] = acc_c[:heads, tap * chans:(tap + 1) * chans]
+    pack_ref[spots[0]:spots[0] + mid, :] = reduce_ref[...]
+    pack_ref[spots[1]:spots[1] + mid, :] = expand_ref[...]
+    for dy in range(3):
+        at_row = spots[2] + dy * mid
+        pack_ref[at_row:at_row + mid, :3 * mid] = spatial_ref[:, dy * 3 * mid:(dy + 1) * 3 * mid]
+
+
+def layout(mid, heads):
+    first = -(-9 * heads // 8) * 8
+    return first, first + mid, first + 2 * mid, first + 5 * mid
+
+
+def piece_rows(s, orders, sizes, total):
+    rows, out = total // len(orders), []
+    for axis in orders[s]:
+        rows //= sizes[axis]
+        out.append(rows)
+    return out
+
+
+def sum_kernel(sizes, orders, pack_ref, stat_ref, out_ref, total_ref, *scratch):
+    subs, depth = len(orders), len(AXES)
+    send, full = scratch[0], scratch[1]
+    recvs = [scratch[2 + s * depth:2 + (s + 1) * depth] for s in range(subs)]
+    stat_send = scratch[2 + subs * depth]
+    stat_recv = scratch[3 + subs * depth:3 + subs * depth + depth]
+    ssem, rsem = scratch[-2:]
+    total = pack_ref.shape[0]
+    share = total // subs
+    me = {axis: lax.axis_index(axis) for axis in AXES}
+    peers = lambda axis: range(1, sizes[axis])
+    mesh_id = pl.DeviceIdType.MESH
+
+    barrier = pltpu.get_barrier_semaphore()
+    for axis in AXES:
+        for d in peers(axis):
+            pl.semaphore_signal(
+                barrier, inc=1, device_id={axis: lax.rem(me[axis] + d, sizes[axis])},
+                device_id_type=mesh_id,
+            )
+    pl.semaphore_wait(barrier, sum(sizes[axis] - 1 for axis in AXES))
+
+    used = [0]
+
+    def push(src, dst, axis, d):
+        n = used[0]
+        used[0] += 1
+        copy = pltpu.make_async_remote_copy(
+            src_ref=src, dst_ref=dst, send_sem=ssem.at[n], recv_sem=rsem.at[n],
+            device_id={axis: lax.rem(me[axis] + d, sizes[axis])}, device_id_type=mesh_id,
+        )
+        copy.start()
+        return copy
+
+    send[...] = pack_ref[...].astype(BF16)
+    base = [s * share for s in range(subs)]
+    held = [None] * subs
+    stat = stat_ref[...]
+    for k in range(depth):
+        copies = []
+        for s in range(subs):
+            axis = orders[s][k]
+            rows = piece_rows(s, orders, sizes, total)[k]
+            for d in peers(axis):
+                to = lax.rem(me[axis] + d, sizes[axis])
+                src = send.at[pl.ds(pl.multiple_of(base[s] + to * rows, 16), rows)]
+                copies.append(push(src, recvs[s][k].at[d - 1], axis, d))
+        stat_send[k] = stat
+        for d in peers(AXES[k]):
+            copies.append(push(stat_send.at[k], stat_recv[k].at[d - 1], AXES[k], d))
+        for copy in copies:
+            copy.wait()
+        for d in peers(AXES[k]):
+            stat = stat + stat_recv[k][d - 1]
+        for s in range(subs):
+            axis = orders[s][k]
+            rows = piece_rows(s, orders, sizes, total)[k]
+            mine = me[axis] * rows
+            if k == 0:
+                got = pack_ref[pl.ds(pl.multiple_of(base[s] + mine, 16), rows), :]
+            else:
+                out_at = pl.ds(pl.multiple_of(base[s] + mine, 16), rows)
+                got = out_ref[out_at, :]
+            for d in peers(axis):
+                got = got + recvs[s][k][d - 1].astype(F32)
+            base[s] = pl.multiple_of(base[s] + mine, 16)
+            where = pl.ds(base[s], rows)
+            if k < depth - 1:
+                out_ref[where, :] = got
+                send[where, :] = got.astype(BF16)
+            else:
+                full[where, :] = got.astype(BF16)
+    total_ref[...] = stat
+    for k in range(depth - 1, -1, -1):
+        copies = []
+        for s in range(subs):
+            axis = orders[s][k]
+            rows = piece_rows(s, orders, sizes, total)[k]
+            where = pl.ds(base[s], rows)
+            for d in peers(axis):
+                copies.append(push(full.at[where], full.at[where], axis, d))
+            base[s] = pl.multiple_of(base[s] - me[axis] * rows, 16)
+        for copy in copies:
+            copy.wait()
+    out_ref[...] = full[...].astype(F32)
+
+
+def sum_devices(pack, stat):
+    sizes = {axis: lax.axis_size(axis) for axis in AXES}
+    orders = [AXES[s:] + AXES[:s] for s in range(len(AXES))]
+    total, chans = pack.shape
+    scratch = [pltpu.VMEM((total, chans), BF16), pltpu.VMEM((total, chans), BF16)]
+    copies = 0
+    for s in range(len(orders)):
+        for axis, rows in zip(orders[s], piece_rows(s, orders, sizes, total)):
+            scratch.append(pltpu.VMEM((max(sizes[axis] - 1, 1), rows, chans), BF16))
+            copies += 2 * (sizes[axis] - 1)
+    scratch.append(pltpu.VMEM((len(AXES),) + stat.shape, F32))
+    for axis in AXES:
+        scratch.append(pltpu.VMEM((max(sizes[axis] - 1, 1),) + stat.shape, F32))
+        copies += sizes[axis] - 1
+    scratch += [pltpu.SemaphoreType.DMA((copies,)), pltpu.SemaphoreType.DMA((copies,))]
+    return pl.pallas_call(
+        functools.partial(sum_kernel, sizes, orders),
+        out_shape=(
+            jax.ShapeDtypeStruct(pack.shape, F32), jax.ShapeDtypeStruct(stat.shape, F32)
+        ),
+        in_specs=[pl.BlockSpec(memory_space=pltpu.VMEM)] * 2,
+        out_specs=[pl.BlockSpec(memory_space=pltpu.VMEM)] * 2,
+        scratch_shapes=scratch,
+        compiler_params=pltpu.CompilerParams(
+            collective_id=0, has_side_effects=True, vmem_limit_bytes=16 * 1024 * 1024
+        ),
+        name="sum_devices",
+    )(pack, stat)
 
 
 def per_device(
@@ -193,9 +341,11 @@
     ones = jnp.ones((tiles, 1, rows, cols), BF16)
     none = jnp.zeros((tiles, 16 - A - 1, rows, cols), BF16)
     field = jnp.concatenate([inputs, code, ones, none], axis=1)
-    field = extended(field, (("row", 2), ("col", 3)), HALO)
-    field = field.reshape(tiles, chans + 16, pixels)
-    field = jnp.pad(field, ((0, 0), (0, 0), (0, length - pixels)))
+    field = extended(field, (("row", 2),), HALO)
+    ends = lax.axis_size("col") - 1
+    left = lax.ppermute(field[..., -HALO:], "col", [(i, i + 1) for i in range(ends)])
+    right = lax.ppermute(field[..., :HALO], "col", [(i + 1, i) for i in range(ends)])
+    field, left, right = (v.transpose(0, 2, 1, 3) for v in (field, left, right))
 
     own = np.zeros((tall, pitch), np.float32)
     own[HALO:HALO + rows, HALO:HALO + cols] = 1.0
@@ -210,19 +360,19 @@
     wc = wide.transpose(2, 0, 1, 3).reshape(outs, 9 * chans)
     wcb = wide.transpose(3, 0, 1, 2).reshape(chans, 9 * outs)
 
+    unit = 16 * len(AXES) * int(np.prod([lax.axis_size(axis) for axis in AXES]))
+    packed = -(-layout(mid, heads)[3] // unit) * unit
+
     call = pl.pallas_call(
-        functools.partial(tile_kernel, pitch, geo),
+        functools.partial(tile_kernel, pitch, geo, heads),
         out_shape=(
-            jax.ShapeDtypeStruct((mid, chans), F32),
-            jax.ShapeDtypeStruct((mid, 9 * mid), F32),
-            jax.ShapeDtypeStruct((chans, mid), F32),
-            jax.ShapeDtypeStruct((9, outs, chans), F32),
-            jax.ShapeDtypeStruct((1, 1), F32),
-            jax.ShapeDtypeStruct((1, 1), F32),
+            jax.ShapeDtypeStruct((packed, chans), F32),
+            jax.ShapeDtypeStruct((8, 128), F32),
         ),
-        in_specs=[pl.BlockSpec(memory_space=pltpu.VMEM)] * 10,
-        out_specs=[pl.BlockSpec(memory_space=pltpu.VMEM)] * 6,
+        in_specs=[pl.BlockSpec(memory_space=pltpu.VMEM)] * 12,
+        out_specs=[pl.BlockSpec(memory_space=pltpu.VMEM)] * 2,
         scratch_shapes=[
+            pltpu.VMEM((chans + 16, length), BF16),
             pltpu.VMEM((mid, length + 2 * EDGE), BF16),
             pltpu.VMEM((mid, length), BF16),
             pltpu.VMEM((chans, length), BF16),
@@ -231,6 +381,9 @@
             pltpu.VMEM((9 * chans, STEP), BF16),
             pltpu.VMEM((9 * mid, STEP), BF16),
             pltpu.VMEM((outs, 9 * chans), F32),
+            pltpu.VMEM((mid, chans), F32),
+            pltpu.VMEM((mid, 9 * mid), F32),
+            pltpu.VMEM((mid, chans), F32),
         ],
         compiler_params=pltpu.CompilerParams(vmem_limit_bytes=50 * 1024 * 1024),
         name="tile_step",
@@ -238,24 +391,25 @@
     sums = None
     for t in range(tiles):
         part = call(
-            field[t], own, spread, reduce_weight, ws, wsb, expand_weight, expand_weight.T, wc, wcb
+            field[t], left[t], right[t], own, spread, reduce_weight, ws, wsb, expand_weight, expand_weight.T, wc, wcb
         )
         sums = part if sums is None else tuple(a + b for a, b in zip(sums, part))
     return finish(sums, mid, heads)
 
 
 def finish(sums, mid, heads):
-    reduce_sum, spatial_sum, expand_sum, class_sum, focal, count = lax.psum(sums, AXES)
-    chans = reduce_sum.shape[1]
-    count = count[0, 0]
+    pack, stat = sum_devices(*sums)
+    chans = pack.shape[1]
+    spots = layout(mid, heads)
+    count = jnp.sum(stat[1])
     scale = 1.0 / count
-    spatial = spatial_sum.reshape(mid, 3, 3, mid).transpose(1, 2, 0, 3)
+    spatial = pack[spots[2]:spots[3], :3 * mid].reshape(3, mid, 3, mid).transpose(0, 2, 1, 3)
     return (
-        focal[0, 0] / count,
-        reduce_sum * scale,
+        jnp.sum(stat[0]) / count,
+        pack[spots[0]:spots[1]] * scale,
         spatial * scale,
-        expand_sum * scale,
-        class_sum[:, :heads].reshape(3, 3, heads, chans) * scale,
+        pack[spots[1]:spots[2]].T * scale,
+        pack[:9 * heads].reshape(3, 3, heads, chans) * scale,
     )
 
 

time: 291 us -> 148 us (0.51)
  waiting for transfers between devices: 101 us -> 6.4 us
  blocking collectives: 43.4 us -> 0 us
  Pallas kernels: 52.9 us -> 93 us
  local copies, waits for them, and re-layouts: 40.6 us -> 22.8 us
  other arithmetic: 25.3 us -> 11.9 us
  between operations: 17.3 us -> 4.03 us
    psum x1 -> x0, waiting for transfers between devices: 91.8 us -> none  [finish(): lax.psum(sums, AXES)]
    psum x1 -> x0, blocking collectives: 43.4 us -> none  [finish(): lax.psum(sums, AXES)]
    pallas_call x1 -> x2, Pallas kernels: 52.9 us -> 93 us  [the longest x1 57.8 us: per_device(): call(field[t], left[t], right[t], own, spread, reduce_weight, ws, wsb, ex...]
    concatenate x2 -> x1, other arithmetic: 18.2 us -> 4.09 us  [extended(): jnp.concatenate([lax.ppermute(tail, axis, [(i, (i + 1) % count) for i in...]
    concatenate x1 -> x0, local copies, waits for them, and re-layouts: 7.74 us -> none  [extended(): jnp.concatenate([lax.ppermute(tail, axis, [(i, (i + 1) % count) for i in...]
    reshape x1 -> x0, local copies, waits for them, and re-layouts: 5.87 us -> none  [per_device(): field = field.reshape(tiles, chans + 16, pixels)]
    squeeze x0 -> x1, other arithmetic: none -> 5.22 us  [per_device(): field[t]]
    mul x3 -> x2, other arithmetic: 4.8 us -> 0.74 us  [the longest x1 0.66 us: finish(): pack[spots[1]:spots[2]].T * scale]
  transfers between devices with their start and end apart: 5 -> 4, of which waited for: 3 -> 2; matrix products, arithmetic and copies ran while one was open for 3% -> 9% of each run, Pallas kernels for 0% -> 0%
where the time goes in v1:
time: 148 us; the launch traced here: 147 us
  Pallas kernels  93 us (63%)
  local copies, waits for them, and re-layouts  22.8 us (15%)
  other arithmetic  11.9 us (8%)
  starting transfers between devices  9.15 us (6%)
  waiting for transfers between devices  6.4 us (4%)
  between operations  4.03 us (3%)
    pallas_call x1, Pallas kernels, per_device(): call(field[t], left[t], right[t], own, spread, reduce_weight, ws, wsb, ex...  57.8 us
    pallas_call x1, Pallas kernels, sum_devices(): pl.pallas_call(functools.partial(sum_kernel, sizes, orders), out_shape=(j...  35.2 us
    slice x2, local copies, waits for them, and re-layouts, per_device(): field[..., :HALO]  6.78 us
    squeeze x1, other arithmetic, per_device(): field[t]  5.22 us
    ppermute x1, starting transfers between devices, extended(): lax.ppermute(tail, axis, [(i, (i + 1) % count) for i in range(ends)])  4.96 us
    concatenate x1, other arithmetic, extended(): jnp.concatenate([lax.ppermute(tail, axis, [(i, (i + 1) % count) for i in...  4.09 us
    ppermute x1, waiting for transfers between devices, extended(): lax.ppermute(head, axis, [((i + 1) % count, i) for i in range(ends)])  3.96 us
    slice x1, local copies, waits for them, and re-layouts, per_device(): field[..., -HALO:]  3.45 us
  transfers between devices with their start and end apart: 4, of which 2 were waited for; matrix products, arithmetic and copies ran while one was open for 9% of the time, Pallas kernels for 0%

profile of v1, /device:TPU:0, one launch (start us, length us, event | category | flops | bytes accessed | tf_op | source)
XLA Modules:
  0.0 147.3 jit_solution(17493835696544950064)
XLA Ops:
  0.7 2.5 %copy.50 = bf16[1,256,32,128]{3,1,2,0:T(8,128)(2,1)S(1)} copy(bf16[1,256,32,128]{3,2,1,0:T(8,128)(2,1)} %param.9) | data formatting | bytes 4194304 | tf_op args[0]
  3.2 0.2 fusion
  3.4 1.0 pad_maximum_fusion.4
  4.4 5.0 %collective-permute-start = (bf16[1,272,4,128]{3,1,2,0:T(8,128)(2,1)}, bf16[1,272,4,128]{3,1,2,0:T(8,128)(2,1)S(1)}, u32[]{:S(2)}, u32[]{:S(2)}) collective-permute-start(bf16[1,272,4,128]{3,1,2,0:T(8,128)(2,1)} %get-tuple-element.32), channel_id=1, source_target_pairs={{0,4},{4,8},{8,12},{1,5},{5,9},{9,13},{2,6},{6,10},{10,14},{3,7},{... | collective-permute-start | bytes 835592 | tf_op jit(solution)/shard_map/ppermute | solution.py:29
  9.4 1.4 collective-permute-start.1
  10.8 0.1 fusion.2
  10.9 0.5 copy.56
  11.4 0.8 reshape.30.wc_ref
  12.2 0.3 copy.60.wcb_ref
  12.6 0.1 copy.55
  12.7 0.1 copy.57.ws_ref
  12.9 0.1 copy.58.wsb_ref
  13.0 0.1 copy.59.we_ref
  13.1 2.4 %collective-permute-done = bf16[1,272,4,128]{3,1,2,0:T(8,128)(2,1)S(1)} collective-permute-done((bf16[1,272,4,128]{3,1,2,0:T(8,128)(2,1)}, bf16[1,272,4,128]{3,1,2,0:T(8,128)(2,1)S(1)}, u32[]{:S(2)}, u32[]{:S(2)}) %collective-permute-start) | collective-permute-done | bytes 278560 | tf_op jit(solution)/shard_map/ppermute | solution.py:29
  15.6 4.0 %collective-permute-done.1 = bf16[1,272,4,128]{3,1,2,0:T(8,128)(2,1)S(1)} collective-permute-done((bf16[1,272,4,128]{3,1,2,0:T(8,128)(2,1)S(1)}, bf16[1,272,4,128]{3,1,2,0:T(8,128)(2,1)S(1)}, u32[]{:S(2)}, u32[]{:S(2)}) %collective-permute-start.1) | collective-permute-done | bytes 278560 | tf_op jit(solution)/shard_map/ppermute | solution.py:31
  19.5 4.1 %pad_maximum_fusion = bf16[1,272,40,128]{3,1,2,0:T(8,128)(2,1)S(1)} fusion(bf16[1,272,4,128]{3,1,2,0:T(8,128)(2,1)S(1)} %collective-permute-done.1, bf16[1,6,32,128]{3,1,2,0:T(8,128)(2,1)S(1)} %broadcast_in_dim.7, bf16[1,1,32,128]{3,1,2,0:T(2,128)(2,1)S(1)} %broadcast_in_dim.6, bf16[1,9,32,128]{3,1,2,0:T(8,128)(2,1)S(1)} %fusion, ...), kind=kLoop, calls=%fused_computation | loop fusion | flops 16711680 | bytes 5570560 | tf_op jit(solution)/shard_map/concatenate | solution.py:27
  23.6 3.3 %fusion.1 = (bf16[1,272,40,4]{3,1,2,0:T(8,128)(2,1)}, bf16[1,272,40,4]{3,1,2,0:T(8,128)(2,1)}) fusion(bf16[1,272,40,128]{3,1,2,0:T(8,128)(2,1)S(1)} %pad_maximum_fusion), kind=kLoop, calls=%fused_computation.15 | loop fusion | bytes 348160 | tf_op jit(solution)/shard_map/slice | solution.py:347
  26.9 3.4 %copy.51 = bf16[1,272,40,4]{1,2,3,0:T(8,128)(2,1)S(1)} copy(bf16[1,272,40,4]{3,1,2,0:T(8,128)(2,1)} %get-tuple-element.31) | data formatting | bytes 174080 | tf_op jit(solution)/shard_map/slice | solution.py:346
  30.4 1.3 collective-permute-start.2
  31.7 3.5 %copy.53 = bf16[1,272,40,4]{1,2,3,0:T(8,128)(2,1)S(1)} copy(bf16[1,272,40,4]{3,1,2,0:T(8,128)(2,1)} %get-tuple-element.30) | data formatting | bytes 174080 | tf_op jit(solution)/shard_map/slice | solution.py:347
  35.2 1.5 %collective-permute-start.3 = (bf16[1,272,40,4]{1,2,3,0:T(8,128)(2,1)S(1)}, bf16[1,272,40,4]{1,2,3,0:T(8,128)(2,1)S(1)}, u32[]{:S(2)}, u32[]{:S(2)}) collective-permute-start(bf16[1,272,40,4]{1,2,3,0:T(8,128)(2,1)S(1)} %copy.53), channel_id=1, source_target_pairs={{1,0},{2,1},{3,2},{5,4},{6,5},{7,6},{9,8},{10,9},{11,10},{13,12},{... | collective-permute-start | bytes 261128 | tf_op jit(solution)/shard_map/ppermute | solution.py:347
  36.6 5.2 %fusion.3.mid_ref = bf16[40,272,128]{2,1,0:T(8,128)(2,1)} fusion(bf16[1,272,4,128]{3,1,2,0:T(8,128)(2,1)S(1)} %collective-permute-done.1, bf16[1,6,32,128]{3,1,2,0:T(8,128)(2,1)S(1)} %broadcast_in_dim.7, bf16[1,1,32,128]{3,1,2,0:T(2,128)(2,1)S(1)} %broadcast_in_dim.6, bf16[1,9,32,128]{3,1,2,0:T(8,128)(2,1)S(1)} %fusion, ...), kind=kLoop, calls=%fused_computation.17 | loop fusion | flops 16711680 | bytes 5570560 | tf_op jit(solution)/shard_map/squeeze | solution.py:394
  41.9 2.9 %copy.52 = bf16[1,272,40,4]{3,1,2,0:T(8,128)(2,1)} copy(bf16[1,272,40,4]{1,2,3,0:T(8,128)(2,1)S(1)} %collective-permute-done.2) | data formatting | bytes 174080 | tf_op jit(solution)/shard_map/ppermute | solution.py:346
  44.7 2.9 %copy.54 = bf16[1,272,40,4]{3,1,2,0:T(8,128)(2,1)} copy(bf16[1,272,40,4]{1,2,3,0:T(8,128)(2,1)S(1)} %collective-permute-done.3) | data formatting | bytes 174080 | tf_op jit(solution)/shard_map/ppermute | solution.py:347
  47.6 57.8 %tile_step.1 = (f32[1536,256]{1,0:T(8,128)S(1)}, f32[8,128]{1,0:T(8,128)S(1)}) custom-call(bf16[40,272,128]{2,1,0:T(8,128)(2,1)} %fusion.3.mid_ref, bf16[40,272,4]{2,1,0:T(8,128)(2,1)} %bitcast.25, bf16[40,272,4]{2,1,0:T(8,128)(2,1)} %bitcast.26, f32[1,5632]{1,0:T(1,128)S(1)} %copy-done.3, bf16[144,16]{1,0:T(8,128)(2,1)S(1)} %copy-done.1, ...), custom_call_target="tpu_custom_call" | custom-call | tf_op jit(solution)/shard_map/tile_step/pallas_call | solution.py:393
  105.4 35.2 %sum_devices.1 = (f32[1536,256]{1,0:T(8,128)S(1)}, f32[8,128]{1,0:T(8,128)S(1)}) custom-call(f32[1536,256]{1,0:T(8,128)S(1)} %get-tuple-element.9.pack_ref, f32[8,128]{1,0:T(8,128)S(1)} %get-tuple-element.10.stat_ref), custom_call_target="tpu_custom_call" | custom-call | tf_op jit(solution)/shard_map/sum_devices/pallas_call | solution.py:304
  140.6 0.6 slice_reduce_fusion
  142.0 0.1 slice_multiply_fusion
  142.1 0.7 multiply_bitcast_fusion
  142.7 1.2 mul.52
  143.9 0.2 mul.46
  144.1 0.7 copy.61
  (23 shorter events, 0.1 us)
Async XLA Ops:
  0.6 2.5 %copy-start.7 = (s32[1,9,32,128]{3,2,1,0:T(8,128)S(1)}, s32[1,9,32,128]{3,2,1,0:T(8,128)}, u32[]{:S(2)}) copy-start(s32[1,9,32,128]{3,2,1,0:T(8,128)} %param.14) | copy-start | bytes 442372
  0.6 2.5 %copy-start.8 = (s32[1,9,32,128]{3,2,1,0:T(8,128)S(1)}, s32[1,9,32,128]{3,2,1,0:T(8,128)}, u32[]{:S(2)}) copy-start(s32[1,9,32,128]{3,2,1,0:T(8,128)} %param.15) | copy-start | bytes 442372
  0.7 10.2 %copy-start.5 = (bf16[3,3,135,256]{3,2,1,0:T(8,128)(2,1)S(1)}, bf16[3,3,135,256]{3,2,1,0:T(8,128)(2,1)}, u32[]{:S(2)}) copy-start(bf16[3,3,135,256]{3,2,1,0:T(8,128)(2,1)} %param.13) | copy-start | bytes 1866244
  3.2 7.8 %copy-start.4 = (bf16[1,256,32,128]{3,1,2,0:T(8,128)(2,1)}, bf16[1,256,32,128]{3,1,2,0:T(8,128)(2,1)S(1)}, u32[]{:S(2)}) copy-start(bf16[1,256,32,128]{3,1,2,0:T(8,128)(2,1)S(1)} %copy.50) | copy-start | bytes 6291460
  4.4 11.2 %collective-permute-start = (bf16[1,272,4,128]{3,1,2,0:T(8,128)(2,1)}, bf16[1,272,4,128]{3,1,2,0:T(8,128)(2,1)S(1)}, u32[]{:S(2)}, u32[]{:S(2)}) collective-permute-start(bf16[1,272,4,128]{3,1,2,0:T(8,128)(2,1)} %get-tuple-element.32), channel_id=1, source_target_pairs={{0,4},{4,8},{8,12},{1,5},{5,9},{9,13},{2,6},{6,10},{10,14},{3,7},{... | collective-permute-start | bytes 835592 | tf_op jit(solution)/shard_map/ppermute | solution.py:29
  9.4 3.2 %copy-start.6 = (bf16[3,3,64,64]{3,2,1,0:T(8,128)(2,1)S(1)}, bf16[3,3,64,64]{3,2,1,0:T(8,128)(2,1)}, u32[]{:S(2)}) copy-start(bf16[3,3,64,64]{3,2,1,0:T(8,128)(2,1)} %param.11) | copy-start | bytes 221188
  9.4 10.1 %collective-permute-start.1 = (bf16[1,272,4,128]{3,1,2,0:T(8,128)(2,1)S(1)}, bf16[1,272,4,128]{3,1,2,0:T(8,128)(2,1)S(1)}, u32[]{:S(2)}, u32[]{:S(2)}) collective-permute-start(bf16[1,272,4,128]{3,1,2,0:T(8,128)(2,1)S(1)} %get-tuple-element.33), channel_id=1, source_target_pairs={{4,0},{8,4},{12,8},{5,1},{9,5},{13,9},{6,2},{10,6},{14,10},{7,3},{... | collective-permute-start | bytes 835592 | tf_op jit(solution)/shard_map/ppermute | solution.py:31
  10.9 2.1 %copy-start = (bf16[256,64]{0,1:T(8,128)(2,1)S(1)}, bf16[256,64]{0,1:T(8,128)(2,1)}, u32[]{:S(2)}) copy-start(bf16[256,64]{0,1:T(8,128)(2,1)} %param.12) | copy-start | bytes 98308
  30.4 11.5 %collective-permute-start.2 = (bf16[1,272,40,4]{1,2,3,0:T(8,128)(2,1)S(1)}, bf16[1,272,40,4]{1,2,3,0:T(8,128)(2,1)S(1)}, u32[]{:S(2)}, u32[]{:S(2)}) collective-permute-start(bf16[1,272,40,4]{1,2,3,0:T(8,128)(2,1)S(1)} %copy.51), channel_id=1, source_target_pairs={{0,1},{1,2},{2,3},{4,5},{5,6},{6,7},{8,9},{9,10},{10,11},{12,13},{... | collective-permute-start | bytes 261128 | tf_op jit(solution)/shard_map/ppermute | solution.py:346
  35.2 9.6 %collective-permute-start.3 = (bf16[1,272,40,4]{1,2,3,0:T(8,128)(2,1)S(1)}, bf16[1,272,40,4]{1,2,3,0:T(8,128)(2,1)S(1)}, u32[]{:S(2)}, u32[]{:S(2)}) collective-permute-start(bf16[1,272,40,4]{1,2,3,0:T(8,128)(2,1)S(1)} %copy.53), channel_id=1, source_target_pairs={{1,0},{2,1},{3,2},{5,4},{6,5},{7,6},{9,8},{10,9},{11,10},{13,12},{... | collective-permute-start | bytes 261128 | tf_op jit(solution)/shard_map/ppermute | solution.py:347
  41.9 5.7 %copy-start.1 = (bf16[144,16]{1,0:T(8,128)(2,1)S(1)}, bf16[144,16]{1,0:T(8,128)(2,1)}, u32[]{:S(2)}) copy-start(bf16[144,16]{1,0:T(8,128)(2,1)} %constant.17.clone.spread_ref) | copy-start | bytes 13828
  41.9 5.7 %copy-start.2 = (bf16[64,256]{1,0:T(8,128)(2,1)S(1)}, bf16[64,256]{1,0:T(8,128)(2,1)}, u32[]{:S(2)}) copy-start(bf16[64,256]{1,0:T(8,128)(2,1)} %wr_ref.1) | copy-start | bytes 98308
  41.9 5.7 %copy-start.3 = (f32[1,5632]{1,0:T(1,128)S(1)}, f32[1,5632]{1,0:T(1,128)}, u32[]{:S(2)}) copy-start(f32[1,5632]{1,0:T(1,128)} %constant.16.clone.own_ref) | copy-start | bytes 67588

commit v2 on v1

--- a/solution.py
+++ b/solution.py
@@ -18,21 +18,106 @@
 AXES = ("dp", "row", "col")
 
 
-def extended(cells, sides, width):
-    for axis, dim in sides:
-        count = lax.axis_size(axis)
-        ends = count - 1
-        head = lax.slice_in_dim(cells, 0, width, axis=dim)
-        tail = lax.slice_in_dim(cells, cells.shape[dim] - width, cells.shape[dim], axis=dim)
-        cells = jnp.concatenate(
-            [
-                lax.ppermute(tail, axis, [(i, (i + 1) % count) for i in range(ends)]),
-                cells,
-                lax.ppermute(head, axis, [((i + 1) % count, i) for i in range(ends)]),
-            ],
-            axis=dim,
+def row_of(mid_ref, top_ref, low_ref, h):
+    rows = mid_ref.shape[0]
+    if h < HALO:
+        return top_ref[h]
+    if h < HALO + rows:
+        return mid_ref[h - HALO]
+    return low_ref[h - HALO - rows]
+
+
+def halo_kernel(
+    sizes, mid_ref, top_ref, low_ref, left_ref, right_ref,
+    got_top, got_low, send_left, send_right, got_left, got_right, ssem, rsem,
+):
+    rows, _, cols = mid_ref.shape
+    tall = rows + 2 * HALO
+    me = {axis: lax.axis_index(axis) for axis in ("row", "col")}
+    mesh_id = pl.DeviceIdType.MESH
+    sides = [(axis, step) for axis in ("row", "col") for step in (1, -1)]
+
+    def exists(axis, step):
+        return me[axis] < sizes[axis] - 1 if step > 0 else me[axis] > 0
+
+    barrier = pltpu.get_barrier_semaphore()
+    for axis, step in sides:
+        @pl.when(exists(axis, step))
+        def _():
+            pl.semaphore_signal(
+                barrier, inc=1, device_id={axis: me[axis] + step}, device_id_type=mesh_id
+            )
+    peers = sum(jnp.where(exists(axis, step), 1, 0) for axis, step in sides)
+    pl.semaphore_wait(barrier, peers)
+
+    def push(n, src, dst, axis, step):
+        copy = pltpu.make_async_remote_copy(
+            src_ref=src, dst_ref=dst, send_sem=ssem.at[n], recv_sem=rsem.at[n],
+            device_id={axis: me[axis] + step}, device_id_type=mesh_id,
         )
-    return cells
+
+        @pl.when(exists(axis, step))
+        def _():
+            copy.start()
+
+        def finish():
+            @pl.when(exists(axis, step))
+            def _():
+                copy.wait_send()
+
+            @pl.when(exists(axis, -step))
+            def _():
+                copy.wait_recv()
+
+            @pl.when(jnp.logical_not(exists(axis, -step)))
+            def _():
+                dst[...] = jnp.zeros(dst.shape, dst.dtype)
+
+        return finish
+
+    down = push(0, mid_ref.at[pl.ds(rows - HALO, HALO)], got_top, "row", 1)
+    up = push(1, mid_ref.at[pl.ds(0, HALO)], got_low, "row", -1)
+
+    def pack(h):
+        cells = row_of(mid_ref, got_top, got_low, h)
+        send_left[:, h * HALO:(h + 1) * HALO] = cells[:, :HALO]
+        send_right[:, h * HALO:(h + 1) * HALO] = cells[:, cols - HALO:]
+
+    send_left[...] = jnp.zeros_like(send_left)
+    send_right[...] = jnp.zeros_like(send_right)
+    for h in range(HALO, HALO + rows):
+        pack(h)
+    down()
+    up()
+    for h in list(range(HALO)) + list(range(HALO + rows, tall)):
+        pack(h)
+    forth = push(2, send_right, got_left, "col", 1)
+    back = push(3, send_left, got_right, "col", -1)
+    top_ref[...] = got_top[...]
+    low_ref[...] = got_low[...]
+    forth()
+    back()
+    left_ref[...] = got_left[...]
+    right_ref[...] = got_right[...]
+
+
+def halos(field):
+    rows, depth, cols = field.shape
+    sizes = {axis: lax.axis_size(axis) for axis in ("row", "col")}
+    lanes = -(-(rows + 2 * HALO) * HALO // 128) * 128
+    band, strip = (HALO, depth, cols), (depth, lanes)
+    return pl.pallas_call(
+        functools.partial(halo_kernel, sizes),
+        out_shape=[jax.ShapeDtypeStruct(v, BF16) for v in (band, band, strip, strip)],
+        in_specs=[pl.BlockSpec(memory_space=pltpu.VMEM)],
+        out_specs=[pl.BlockSpec(memory_space=pltpu.VMEM)] * 4,
+        scratch_shapes=[pltpu.VMEM(v, BF16) for v in (band, band, strip, strip, strip, strip)]
+        + [pltpu.SemaphoreType.DMA((4,)), pltpu.SemaphoreType.DMA((4,))],
+        compiler_params=pltpu.CompilerParams(
+            collective_id=1, has_side_effects=True, vmem_limit_bytes=16 * 1024 * 1024
+        ),
+        name="halos",
+    )(field)
 
 
 def dot(a, b):
@@ -45,7 +130,7 @@
 
 def tile_kernel(
     pitch, geo, heads_in,
-    mid_ref, left_ref, right_ref, own_ref, spread_ref, wr_ref, ws_ref, wsb_ref, we_ref, wet_ref, wc_ref, wcb_ref,
+    mid_ref, top_ref, low_ref, left_ref, right_ref, own_ref, spread_ref, wr_ref, ws_ref, wsb_ref, we_ref, wet_ref, wc_ref, wcb_ref,
     pack_ref, stat_ref,
     x_ref, first, second, block, dlog, dsec, big, small, acc_c, reduce_ref, spatial_ref, expand_ref,
 ):
@@ -68,14 +153,17 @@
     def loop(start, steps, body, init=0):
         return lax.fori_loop(0, steps, lambda i, c: body(at(i, start), c), init)
 
-    tall, _, cols = mid_ref.shape
+    rows, _, cols = mid_ref.shape
+    tall = rows + 2 * HALO
     x_ref[:, tall * pitch // 128 * 128:] = jnp.zeros(
         (x_ref.shape[0], length - tall * pitch // 128 * 128), BF16
     )
     for h in range(tall):
-        x_ref[:, h * pitch:h * pitch + HALO] = left_ref[h]
-        x_ref[:, h * pitch + HALO:h * pitch + HALO + cols] = mid_ref[h]
-        x_ref[:, h * pitch + HALO + cols:(h + 1) * pitch] = right_ref[h]
+        x_ref[:, h * pitch:h * pitch + HALO] = left_ref[:, h * HALO:(h + 1) * HALO]
+        x_ref[:, h * pitch + HALO:h * pitch + HALO + cols] = row_of(
+            mid_ref, top_ref, low_ref, h
+        )
+        x_ref[:, h * pitch + HALO + cols:(h + 1) * pitch] = right_ref[:, h * HALO:(h + 1) * HALO]
 
     first[:, :EDGE] = jnp.zeros((mid, EDGE), BF16)
     first[:, EDGE + length:] = jnp.zeros((mid, EDGE), BF16)
@@ -341,11 +429,7 @@
     ones = jnp.ones((tiles, 1, rows, cols), BF16)
     none = jnp.zeros((tiles, 16 - A - 1, rows, cols), BF16)
     field = jnp.concatenate([inputs, code, ones, none], axis=1)
-    field = extended(field, (("row", 2),), HALO)
-    ends = lax.axis_size("col") - 1
-    left = lax.ppermute(field[..., -HALO:], "col", [(i, i + 1) for i in range(ends)])
-    right = lax.ppermute(field[..., :HALO], "col", [(i + 1, i) for i in range(ends)])
-    field, left, right = (v.transpose(0, 2, 1, 3) for v in (field, left, right))
+    field = field.transpose(0, 2, 1, 3)
 
     own = np.zeros((tall, pitch), np.float32)
     own[HALO:HALO + rows, HALO:HALO + cols] = 1.0
@@ -369,7 +453,7 @@
             jax.ShapeDtypeStruct((packed, chans), F32),
             jax.ShapeDtypeStruct((8, 128), F32),
         ),
-        in_specs=[pl.BlockSpec(memory_space=pltpu.VMEM)] * 12,
+        in_specs=[pl.BlockSpec(memory_space=pltpu.VMEM)] * 14,
         out_specs=[pl.BlockSpec(memory_space=pltpu.VMEM)] * 2,
         scratch_shapes=[
             pltpu.VMEM((chans + 16, length), BF16),
@@ -391,7 +475,7 @@
     sums = None
     for t in range(tiles):
         part = call(
-            field[t], left[t], right[t], own, spread, reduce_weight, ws, wsb, expand_weight, expand_weight.T, wc, wcb
+            field[t], *halos(field[t]), own, spread, reduce_weight, ws, wsb, expand_weight, expand_weight.T, wc, wcb
         )
         sums = part if sums is None else tuple(a + b for a, b in zip(sums, part))
     return finish(sums, mid, heads)

time: 148 us -> 125 us (0.84)
  Pallas kernels: 93 us -> 106 us
  local copies, waits for them, and re-layouts: 22.8 us -> 12 us
  starting transfers between devices: 9.15 us -> 0 us
  other arithmetic: 11.9 us -> 3.18 us
  waiting for transfers between devices: 6.4 us -> 0 us
    pallas_call x1 -> x2, Pallas kernels: 57.8 us -> 70.5 us  [the longest x1 57 us: per_device(): call(field[t], *halos(field[t]), own, spread, reduce_weight, ws, wsb, exp...]
    slice x3 -> x0, local copies, waits for them, and re-layouts: 10.2 us -> none  [the longest x2 6.78 us: per_device(): field[..., :HALO]]
    ppermute x4 -> x0, starting transfers between devices: 9.15 us -> none  [the longest x1 4.96 us: extended(): lax.ppermute(tail, axis, [(i, (i + 1) % count) for i in range(ends)])]
    ppermute x4 -> x0, waiting for transfers between devices: 6.4 us -> none  [the longest x1 3.96 us: extended(): lax.ppermute(head, axis, [((i + 1) % count, i) for i in range(ends)])]
    ppermute x2 -> x0, local copies, waits for them, and re-layouts: 5.73 us -> none  [the longest x1 2.87 us: per_device(): lax.ppermute(field[..., :HALO], 'col', [(i + 1, i) for i in range(ends)])]
    squeeze x1, other arithmetic: 5.22 us -> 0.65 us  [per_device(): field[t]]
    concatenate x1 -> x0, other arithmetic: 4.09 us -> none  [extended(): jnp.concatenate([lax.ppermute(tail, axis, [(i, (i + 1) % count) for i in...]
    unnamed x21 -> x15, local copies, waits for them, and re-layouts: 3.37 us -> 5.45 us
  transfers between devices with their start and end apart: 4 -> 0, of which waited for: 2 -> 0; matrix products, arithmetic and copies ran while one was open for 9% -> 0% of each run, Pallas kernels for 0% -> 0%
where the time goes in v2:
time: 125 us
  Pallas kernels  106 us (85%)
  local copies, waits for them, and re-layouts  12 us (10%)
  between operations  3.95 us (3%)
  other arithmetic  3.18 us (3%)
    pallas_call x1, Pallas kernels, per_device(): call(field[t], *halos(field[t]), own, spread, reduce_weight, ws, wsb, exp...  57 us
    pallas_call x1, Pallas kernels, sum_devices(): pl.pallas_call(functools.partial(sum_kernel, sizes, orders), out_shape=(j...  35 us
    pallas_call x1, Pallas kernels, halos(): pl.pallas_call(functools.partial(halo_kernel, sizes), out_shape=[jax.Shap...  13.4 us
    unnamed x15, local copies, waits for them, and re-layouts  5.45 us

profile of v2, /device:TPU:0, one launch (start us, length us, event | category | flops | bytes accessed | tf_op | source)
XLA Modules:
  0.0 124.6 jit_solution(6426291032104191624)
XLA Ops:
  0.6 0.1 pad.8.clone
  0.7 0.1 pad.7.clone
  0.8 0.9 copy.41.we_ref
  1.7 1.0 copy.40.wsb_ref
  2.7 1.2 fusion
  3.9 1.0 copy.37
  4.9 0.1 copy.39.ws_ref
  5.1 1.2 fusion.1
  6.2 0.3 copy.42.wcb_ref
  6.6 0.5 copy.38
  7.1 0.8 reshape.30.wc_ref
  7.9 2.4 %copy.36 = bf16[1,256,32,128]{3,1,2,0:T(8,128)(2,1)S(1)} copy(bf16[1,256,32,128]{3,2,1,0:T(8,128)(2,1)} %param.9) | data formatting | bytes 4194304 | tf_op args[0]
  10.3 0.6 maximum_bitcast_fusion.mid_ref
  10.9 0.0 copy-start
  10.9 0.0 copy-start.2
  10.9 0.0 copy-start.3
  11.0 0.0 copy-start.4
  11.0 0.0 copy-start.5
  11.0 13.4 %halos.1 = (bf16[4,272,128]{2,1,0:T(8,128)(2,1)S(1)}, bf16[4,272,128]{2,1,0:T(8,128)(2,1)S(1)}, bf16[272,256]{1,0:T(8,128)(2,1)S(1)}, bf16[272,256]{1,0:T(8,128)(2,1)S(1)}) custom-call(bf16[32,272,128]{2,1,0:T(8,128)(2,1)S(1)} %maximum_bitcast_fusion.mid_ref), custom_call_target="tpu_custom_call" | custom-call | tf_op jit(solution)/shard_map/halos/pallas_call | solution.py:109
  24.4 0.0 copy-done
  24.4 0.0 copy-done.2
  24.4 0.0 copy-done.3
  24.5 0.0 copy-done.4
  24.5 57.0 %tile_step.1 = (f32[1536,256]{1,0:T(8,128)}, f32[8,128]{1,0:T(8,128)S(1)}) custom-call(bf16[32,272,128]{2,1,0:T(8,128)(2,1)} %copy-done, bf16[4,272,128]{2,1,0:T(8,128)(2,1)S(1)} %get-tuple-element.13.top_ref, bf16[4,272,128]{2,1,0:T(8,128)(2,1)S(1)} %get-tuple-element.14.low_ref, bf16[272,256]{1,0:T(8,128)(2,1)S(1)} %get-tuple-element.15.left_ref, ...), custom_call_target="tpu_custom_call" | custom-call | tf_op jit(solution)/shard_map/tile_step/pallas_call | solution.py:477
  81.5 1.4 %copy-done.1 = f32[1536,256]{1,0:T(8,128)S(1)} copy-done((f32[1536,256]{1,0:T(8,128)S(1)}, f32[1536,256]{1,0:T(8,128)}, u32[]{:S(2)}) %copy-start.1) | copy-done | bytes 1572888
  82.9 35.0 %sum_devices.1 = (f32[1536,256]{1,0:T(8,128)S(1)}, f32[8,128]{1,0:T(8,128)S(1)}) custom-call(f32[1536,256]{1,0:T(8,128)S(1)} %copy-done.1, f32[8,128]{1,0:T(8,128)S(1)} %get-tuple-element.18.stat_ref), custom_call_target="tpu_custom_call" | custom-call | tf_op jit(solution)/shard_map/sum_devices/pallas_call | solution.py:392
  118.0 0.6 slice_reduce_fusion
  120.6 0.7 multiply_bitcast_fusion
  121.3 0.1 slice_multiply_fusion
  121.4 1.2 mul.52
  122.5 0.2 mul.46
  122.7 0.7 copy.43
  (4 shorter events, 0.0 us)
Async XLA Ops:
  10.9 13.5 %copy-start = (bf16[32,272,128]{2,1,0:T(8,128)(2,1)}, bf16[32,272,128]{2,1,0:T(8,128)(2,1)S(1)}, u32[]{:S(2)}) copy-start(bf16[32,272,128]{2,1,0:T(8,128)(2,1)S(1)} %maximum_bitcast_fusion.mid_ref) | copy-start | bytes 6684676
  10.9 13.5 %copy-start.2 = (bf16[256,64]{0,1:T(8,128)(2,1)S(1)}, bf16[256,64]{0,1:T(8,128)(2,1)}, u32[]{:S(2)}) copy-start(bf16[256,64]{0,1:T(8,128)(2,1)} %param.12) | copy-start | bytes 98308
  10.9 13.5 %copy-start.3 = (bf16[144,16]{1,0:T(8,128)(2,1)S(1)}, bf16[144,16]{1,0:T(8,128)(2,1)}, u32[]{:S(2)}) copy-start(bf16[144,16]{1,0:T(8,128)(2,1)} %constant.17.clone.spread_ref) | copy-start | bytes 13828
  11.0 13.5 %copy-start.4 = (bf16[64,256]{1,0:T(8,128)(2,1)S(1)}, bf16[64,256]{1,0:T(8,128)(2,1)}, u32[]{:S(2)}) copy-start(bf16[64,256]{1,0:T(8,128)(2,1)} %wr_ref.1) | copy-start | bytes 98308
  11.0 13.5 %copy-start.5 = (f32[1,5632]{1,0:T(1,128)S(1)}, f32[1,5632]{1,0:T(1,128)}, u32[]{:S(2)}) copy-start(f32[1,5632]{1,0:T(1,128)} %constant.16.clone.own_ref) | copy-start | bytes 67588
  81.5 1.4 %copy-start.1 = (f32[1536,256]{1,0:T(8,128)S(1)}, f32[1536,256]{1,0:T(8,128)}, u32[]{:S(2)}) copy-start(f32[1536,256]{1,0:T(8,128)} %get-tuple-element.17.pack_ref) | copy-start | bytes 4718596
